TPU v7x, 32 devices: a whole 2x2x4 slice. The times are simulated.
32 devices in a mesh: wide: 16 (over z, y, x), cols: 2 (over core).
Axes of the slice: x: 2, y: 2, z: 4, core: 2. Of those that a mesh axis runs over, the one named last changes fastest.
Arguments:
- factor: float32 [32768, 256], P('wide', 'cols')
- gates: float32 [8, 128, 128], replicated, may hold values from -0.5 to 0.5
- gate_layout: int32 [256], P('wide'), may hold values from 0 to 7
- jump_masks: int32 [3], replicated, may hold values from 1 to 15
- jump_rates: float32 [3], replicated, may hold values from 0.1 to 0.4
- sketch_perm: int32 [1024], replicated, may hold values from 0 to 1023, each once
- bases: float32 [8, 64, 64], replicated, may hold values from -0.75 to 0.75
- basis_index: int32 [16, 32], P('wide'), may hold values from 0 to 7
Outputs:
- new_factor: float32 [32768, 256], P('wide', 'cols')
- weights: float32 [16, 2048], P('wide', 'cols')
Inputs may be any that keep to these rules, and one draw needn't show every extreme that they name: `jump_masks`: nonzero bit masks over the high qubits. `sketch_perm`: each value appears once.
All inputs are finite; a program needn't handle non-finite values.
Results may differ from a plain program's by a relative error of at most 0.0003.
Values sent between devices are 32-bit elements; how exact they have to be, the bound alone decides.
A program may use at most 64 MiB of HBM per device.

v0:
```python
import functools

import jax
import jax.numpy as jnp
from jax import lax
from jax.experimental import pallas as pl
from jax.experimental.pallas import tpu as pltpu
from jax.sharding import PartitionSpec as P

NS_ITERS = 7
MESH = pl.DeviceIdType.MESH
VMEM = pl.BlockSpec(memory_space=pltpu.VMEM)
SMEM = pl.BlockSpec(memory_space=pltpu.SMEM)
HBM = pl.BlockSpec(memory_space=pltpu.HBM)
LIMIT = 48 * 1024 * 1024
NN = (((1,), (0,)), ((), ()))
TN = (((0,), (0,)), ((), ()))
NT = (((1,), (1,)), ((), ()))


def split2(x):
    high = x.astype(jnp.bfloat16)
    return high, (x - high.astype(jnp.float32)).astype(jnp.bfloat16)


def split3(x):
    high = x.astype(jnp.bfloat16)
    rest = x - high.astype(jnp.float32)
    middle = rest.astype(jnp.bfloat16)
    return high, middle, (rest - middle.astype(jnp.float32)).astype(jnp.bfloat16)


def bdot(a, b, dims):
    return lax.dot_general(a, b, dims, preferred_element_type=jnp.float32)


def dot3(a, b, dims=NN):
    ah, al = a if isinstance(a, tuple) else split2(a)
    bh, bl = b if isinstance(b, tuple) else split2(b)
    return bdot(ah, bh, dims) + (bdot(ah, bl, dims) + bdot(al, bh, dims))


def remote(src, dst, send_sem, recv_sem, device):
    return pltpu.make_async_remote_copy(
        src_ref=src, dst_ref=dst, send_sem=send_sem, recv_sem=recv_sem, device_id=device, device_id_type=MESH
    )


def exchange_kernel(
    count, layout_ref, perm_ref, gates_ref, factor_ref, moved_ref, table_ref,
    held_gates, held, gated, layout, load_sem, send_sem, recv_sem, pass_sem, got_sem,
):
    me = lax.axis_index("wide")
    col = lax.axis_index("cols")
    partner = (me, 1 - col)
    rows, width = held.shape
    order = held_gates.shape[1]
    lows = rows // count
    blocks = rows // order
    load_gates = pltpu.make_async_copy(gates_ref, held_gates, load_sem.at[0])
    load_factor = pltpu.make_async_copy(factor_ref, held, load_sem.at[1])
    load_layout = pltpu.make_async_copy(layout_ref, layout, load_sem.at[2])
    load_layout.start()
    load_gates.start()
    load_factor.start()
    barrier = pltpu.get_barrier_semaphore()

    def signal(d, carry):
        pl.semaphore_signal(barrier, inc=1, device_id=(lax.rem(me + d, count), col), device_id_type=MESH)
        return carry

    lax.fori_loop(1, count, signal, 0)
    pl.semaphore_signal(barrier, inc=1, device_id=partner, device_id_type=MESH)

    def outgoing(h):
        at = pl.ds(pl.multiple_of(h * lows, lows), lows)
        return remote(gated.at[at, :], moved_ref.at[col, me], send_sem.at[h], recv_sem.at[me], (h, col))

    def forward(s):
        return remote(moved_ref.at[col, s], moved_ref.at[col, s], pass_sem.at[s], got_sem.at[s], partner)

    per = order // lows
    unroll = 4 if blocks % 4 == 0 else 1
    first = me // per + 1

    def gate(i):
        for u in range(unroll):
            b = lax.rem(first + i * unroll + u, blocks)
            at = pl.ds(pl.multiple_of(b * order, order), order)
            gated[at, :] = dot3(held_gates[layout[b]], held[at, :])

    def send(i):
        for u in range(unroll):
            b = lax.rem(first + i * unroll + u, blocks)
            for j in range(per):
                h = b * per + j

                @pl.when(h != me)
                def _():
                    outgoing(h).start()

    load_layout.wait()
    load_gates.wait()
    load_factor.wait()
    gate(0)
    pl.semaphore_wait(barrier, count)

    def step(i, carry):
        gate(i)
        send(i - 1)
        return carry

    lax.fori_loop(1, blocks // unroll, step, 0)
    send(blocks // unroll - 1)
    own = pl.ds(pl.multiple_of(me * lows, lows), lows)
    moved_ref[col, me] = gated[own, :]
    remote(gated.at[own, :], moved_ref.at[col, me], pass_sem.at[me], got_sem.at[me], partner).start()

    rank, stacked = table_ref.shape
    perm = perm_ref[...]
    strip = 64
    for r in range(0, rank, strip):
        target = lax.broadcasted_iota(jnp.int32, (strip, stacked), 0) + r
        piece = jnp.zeros((strip, stacked), jnp.float32)
        for k in range(stacked // rank):
            piece = jnp.where(perm == target + k * rank, 1.0 - 2.0 * (k % 2), piece)
        table_ref[r:r + strip, :] = piece.astype(jnp.bfloat16)

    def relay(i, carry):
        s = lax.rem(me + count - i, count)
        arrived = moved_ref.at[col, s]
        remote(arrived, arrived, send_sem.at[s], recv_sem.at[s], (s, col)).wait_recv()
        forward(s).start()
        return carry

    lax.fori_loop(1, count, relay, 0)

    def drain(d, carry):
        outgoing(lax.rem(me + d, count)).wait_send()
        return carry

    lax.fori_loop(1, count, drain, 0)

    def finish(d, carry):
        s = lax.rem(me + count - d, count)
        forward(s).wait_send()
        remote(moved_ref.at[1 - col, s], moved_ref.at[1 - col, s], pass_sem.at[s], got_sem.at[s], partner).wait_recv()
        return carry

    lax.fori_loop(0, count, finish, 0)


def sketch_kernel(
    groups, mask_ref, rate_ref, moved_ref, table_ref, sketch_ref, full_ref,
    high, low, part, inbox, sums, lanes, masks, rates_held, load_sem,
    near_send, near_recv, far_send, far_recv, out_send, out_recv, spread_send, spread_recv, pass_sem, got_sem,
):
    me = lax.axis_index("wide")
    col = lax.axis_index("cols")
    partner = (me, 1 - col)
    near, far = part.shape[:2]
    p = lax.rem(me, near)
    o = me // near

    def beside(i):
        return lax.rem(p + i, near)

    def beyond(i):
        return lax.rem(o + i, far)

    def device(there, q):
        return (there * near + q, col)

    load_masks = pltpu.make_async_copy(mask_ref, masks, load_sem.at[0])
    load_rates = pltpu.make_async_copy(rate_ref, rates_held, load_sem.at[1])
    load_masks.start()
    load_rates.start()
    barrier = pltpu.get_barrier_semaphore()
    for i in range(1, near):
        pl.semaphore_signal(barrier, inc=1, device_id=device(o, beside(i)), device_id_type=MESH)
    for i in range(1, far):
        pl.semaphore_signal(barrier, inc=1, device_id=device(beyond(i), p), device_id_type=MESH)
    pl.semaphore_signal(barrier, inc=1, device_id=partner, device_id_type=MESH)

    halves, count, lows, width = moved_ref.shape
    rows, stacked = high.shape
    rank = halves * width
    terms = stacked // rank
    load_masks.wait()
    load_rates.wait()
    rates = [rates_held[k] for k in range(terms - 1)]
    coefs = [jnp.full((1, width), 1.0 - 0.5 * sum(rates), jnp.float32)]
    coefs += [jnp.sqrt(jnp.full((1, width), rate, jnp.float32)) for rate in rates]

    def fill(w, carry):
        at = pl.ds(pl.multiple_of(w * lows, lows), lows)
        for k in range(terms):
            source = w if k == 0 else jnp.bitwise_xor(w, masks[k - 1])
            for half in range(halves):
                top, rest = split2(coefs[k] * moved_ref[half, source])
                columns = slice(k * rank + half * width, k * rank + (half + 1) * width)
                high[at, columns] = top
                low[at, columns] = rest
        return carry

    lax.fori_loop(0, count, fill, 0)
    tile = min(rows, 512)
    for t in range(rows // tile):
        at = slice(t * tile, (t + 1) * tile)
        sketch_ref[at, :] = bdot(high[at, :], table_ref[...], NT) + bdot(low[at, :], table_ref[...], NT)
    mine = split2(sketch_ref[:, pl.ds(pl.multiple_of(col * width, width), width)])
    deep, wide = part.shape[2:]
    step = min(wide, rank)
    for k in range(terms):
        columns = slice(k * rank, (k + 1) * rank)
        value = dot3(mine, (high[:, columns], low[:, columns]), TN)
        pieces = []
        for g in range(k * rank // wide, max(k * rank // wide + 1, (k + 1) * rank // wide)):
            start = max(0, k * rank - g * wide)
            for r in range(width // deep):
                q, there = divmod(r * groups + g, far)
                left = g * wide + start - k * rank
                part[q, there, :, start:start + step] = value[r * deep:(r + 1) * deep, left:left + step]
            pieces.append((g, start))
        if k == 0:
            pl.semaphore_wait(barrier, near + far - 1)
        for g, start in pieces:
            for r in range(width // deep):
                q, there = divmod(r * groups + g, far)

                @pl.when(q != p)
                def _():
                    remote(
                        part.at[q, there, :, start:start + step], inbox.at[p, there, :, start:start + step],
                        near_send.at[q, there], near_recv.at[p, there], device(o, q),
                    ).start()

    def near_copy(q, there):
        return remote(part.at[q, there], inbox.at[p, there], near_send.at[q, there], near_recv.at[p, there], device(o, q))

    def far_copy(there):
        return remote(sums.at[there], lanes.at[o], far_send.at[there], far_recv.at[o], device(there, p))

    for j in range(1, far + 1):
        there = beyond(j)
        value = part[p, there]
        for i in range(1, near):
            q = beside(i)
            remote(
                inbox.at[q, there], inbox.at[q, there], near_send.at[q, there], near_recv.at[q, there], device(o, q)
            ).wait_recv()
            value = value + inbox[q, there]
        sums[there] = value
        if j < far:
            far_copy(there).start()
    value = sums[o]
    for j in range(1, far):
        there = beyond(j)
        remote(lanes.at[there], lanes.at[there], far_send.at[there], far_recv.at[there], device(there, p)).wait_recv()
        value = value + lanes[there]
    full_ref[col, p, o] = value
    for j in range(1, far + 1):
        for i in range(1, near):
            near_copy(beside(i), beyond(j)).wait_send()
    for j in range(1, far):
        far_copy(beyond(j)).wait_send()

    def out_copy(there):
        return remote(full_ref.at[col, p, o], full_ref.at[col, p, o], out_send.at[there], out_recv.at[o], device(there, p))

    def spread_copy(q, there):
        block = full_ref.at[col, p, there]
        return remote(block, block, spread_send.at[q, there], spread_recv.at[p, there], device(o, q))

    def pass_copy(q, there):
        block = full_ref.at[col, q, there]
        return remote(block, block, pass_sem.at[q, there], got_sem.at[q, there], partner)

    def spread(there):
        for i in range(1, near):
            spread_copy(beside(i), there).start()
        pass_copy(p, there).start()

    for j in range(1, far):
        out_copy(beyond(j)).start()
    spread(o)
    for j in range(1, far):
        there = lax.rem(o + far - j, far)
        block = full_ref.at[col, p, there]
        remote(block, block, out_send.at[there], out_recv.at[there], device(there, p)).wait_recv()
        spread(there)
    for j in range(far):
        there = lax.rem(o + far - j, far)
        for i in range(1, near):
            q = lax.rem(p + near - i, near)
            block = full_ref.at[col, q, there]
            remote(block, block, spread_send.at[q, there], spread_recv.at[q, there], device(o, q)).wait_recv()
            pass_copy(q, there).start()
    for j in range(1, far):
        out_copy(beyond(j)).wait_send()
    for j in range(far):
        there = lax.rem(o + far - j, far)
        for i in range(1, near):
            spread_copy(beside(i), there).wait_send()
        for i in range(near):
            q = lax.rem(p + near - i, near)
            pass_copy(q, there).wait_send()
            block = full_ref.at[1 - col, q, there]
            remote(block, block, pass_sem.at[q, there], got_sem.at[q, there], partner).wait_recv()


def newton_root(mat, eye, need_inverse):
    fro = jnp.sqrt(jnp.sum(mat * mat))
    approx = mat / (fro + 1e-06)
    middle = 1.5 * eye - 0.5 * approx
    approx = dot3(approx, middle)
    inverse = middle
    for step in range(1, NS_ITERS):
        inv2 = split2(inverse)
        app2 = split2(approx)
        mid2 = split2(1.5 * eye - 0.5 * dot3(inv2, app2))
        last = step == NS_ITERS - 1
        if not (last and need_inverse):
            approx = dot3(app2, mid2)
        if not last or need_inverse:
            inverse = dot3(mid2, inv2)
    return (inverse if need_inverse else approx), fro


def finish_kernel(index_ref, proj_ref, table_ref, sketch_ref, bases_ref, new_ref, weight_ref, fresh, squares, store_sem):
    col = lax.axis_index("cols")
    rank = proj_ref.shape[0]
    rows = sketch_ref.shape[0]
    width = new_ref.shape[1]
    rot = bases_ref.shape[1]
    row = lax.broadcasted_iota(jnp.int32, (rank, rank), 0)
    column = lax.broadcasted_iota(jnp.int32, (rank, rank), 1)
    eye = jnp.where(row == column, 1.0, 0.0).astype(jnp.float32)
    proj = proj_ref[...]
    ph, pm, plow = split3(proj)
    table = table_ref[...]
    gram = bdot(ph, table, NT) + (bdot(pm, table, NT) + bdot(plow, table, NT))
    inverse, _ = newton_root(gram, eye, True)
    inv2 = split2(inverse)
    coeff = split2(dot3(inv2, (ph, pm), TN))
    core = dot3(coeff, coeff, NT)
    approx, fro = newton_root(core, eye, False)
    mixing = split2(dot3(inv2, split2(jnp.sqrt(fro + 1e-06) * approx)))
    tile = min(rows, 512)
    mine = pl.ds(pl.multiple_of(col * width, width), width)
    stores = []
    for t in range(rows // tile):
        at = slice(t * tile, (t + 1) * tile)
        fresh[at, :] = dot3(sketch_ref[at, :], mixing)
        store = pltpu.make_async_copy(fresh.at[at, mine], new_ref.at[at, :], store_sem.at[t])
        store.start()
        stores.append(store)
    share = squares.shape[0]
    for i in range(share // rot):
        start = pl.multiple_of(col * share + i * rot, rot)
        turned = dot3(bases_ref[index_ref[col * (share // rot) + i]], fresh[pl.ds(start, rot), :])
        squares[i * rot:(i + 1) * rot, :] = turned * turned
    ones = jnp.ones((8, rank), jnp.bfloat16)
    sh, sm, sl = split3(squares[...])
    sums = bdot(ones, sh, NT) + (bdot(ones, sm, NT) + bdot(ones, sl, NT))
    weight_ref[...] = sums[0:1, :] / rank
    for store in stores:
        store.wait()


def per_device(factor, gates, gate_layout, jump_masks, jump_rates, sketch_perm, bases, basis_index):
    rows, width = factor.shape
    count = lax.axis_size("wide")
    halves = lax.axis_size("cols")
    rank = width * halves
    stacked = sketch_perm.shape[0]
    lows = rows // count
    f32 = jnp.float32
    bf16 = jnp.bfloat16

    def dma(*shape):
        return pltpu.SemaphoreType.DMA(shape)

    moved, table = pl.pallas_call(
        functools.partial(exchange_kernel, count),
        out_shape=[
            jax.ShapeDtypeStruct((halves, count, lows, width), f32),
            jax.ShapeDtypeStruct((rank, stacked), bf16),
        ],
        in_specs=[HBM, VMEM, HBM, HBM],
        out_specs=[VMEM, VMEM],
        scratch_shapes=[
            pltpu.VMEM(gates.shape, f32),
            pltpu.VMEM((rows, width), f32),
            pltpu.VMEM((rows, width), f32),
            pltpu.SMEM(gate_layout.shape, jnp.int32),
            dma(3), dma(count), dma(count), dma(count), dma(count),
        ],
        compiler_params=pltpu.CompilerParams(collective_id=0, has_side_effects=True, vmem_limit_bytes=LIMIT),
        name="exchange",
    )(gate_layout, sketch_perm.reshape(1, stacked), gates, factor)

    deep = max(8, width // count)
    groups = count * deep // width
    wide = stacked // groups
    near = 1
    while near * near * 4 <= count:
        near *= 2
    far = count // near
    sketch, full = pl.pallas_call(
        functools.partial(sketch_kernel, groups),
        out_shape=[
            jax.ShapeDtypeStruct((rows, rank), f32),
            jax.ShapeDtypeStruct((halves, near, far, deep, wide), f32),
        ],
        in_specs=[HBM, HBM, VMEM, VMEM],
        out_specs=[VMEM, VMEM],
        scratch_shapes=[
            pltpu.VMEM((rows, stacked), bf16),
            pltpu.VMEM((rows, stacked), bf16),
            pltpu.VMEM((near, far, deep, wide), f32),
            pltpu.VMEM((near, far, deep, wide), f32),
            pltpu.VMEM((far, deep, wide), f32),
            pltpu.VMEM((far, deep, wide), f32),
            pltpu.SMEM(jump_masks.shape, jnp.int32),
            pltpu.SMEM(jump_rates.shape, f32),
            dma(2), dma(near, far), dma(near, far), dma(far), dma(far), dma(far), dma(far),
            dma(near, far), dma(near, far), dma(near, far), dma(near, far),
        ],
        compiler_params=pltpu.CompilerParams(collective_id=1, has_side_effects=True, vmem_limit_bytes=LIMIT),
        name="sketch",
    )(jump_masks, jump_rates, moved, table)
    proj = full.reshape(halves, count // groups, groups, deep, wide).transpose(0, 1, 3, 2, 4).reshape(rank, stacked)

    return pl.pallas_call(
        finish_kernel,
        out_shape=[
            jax.ShapeDtypeStruct((rows, width), f32),
            jax.ShapeDtypeStruct((1, rows // halves), f32),
        ],
        in_specs=[SMEM, VMEM, VMEM, VMEM, VMEM],
        out_specs=[HBM, VMEM],
        scratch_shapes=[
            pltpu.VMEM((rows, rank), f32),
            pltpu.VMEM((rows // halves, rank), f32),
            dma(max(1, rows // 512)),
        ],
        compiler_params=pltpu.CompilerParams(vmem_limit_bytes=LIMIT),
        name="finish",
    )(basis_index.reshape(-1), proj, table, sketch, bases)


def solution(mesh):
    return jax.shard_map(
        per_device,
        mesh=mesh,
        in_specs=(P("wide", "cols"), P(), P("wide"), P(), P(), P(), P(), P("wide", None)),
        out_specs=(P("wide", "cols"), P("wide", "cols")),
        check_vma=False,
    )
```

profile of v0, /device:TPU:0, one launch (start us, length us, event | category | flops | bytes accessed | tf_op | source)
XLA Modules:
  0.0 82.0 jit_solution(5380435157339286767)
XLA Ops:
  0.6 0.0 copy-start
  0.6 1.2 %copy-done = f32[2048,128]{1,0:T(8,128)S(1)} copy-done((f32[2048,128]{1,0:T(8,128)S(1)}, f32[2048,128]{1,0:T(8,128)}, u32[]{:S(2)}) %copy-start) | copy-done | bytes 1048600
  1.9 0.0 copy-start.1
  1.9 1.0 %copy-done.1 = f32[8,128,128]{2,1,0:T(8,128)S(1)} copy-done((f32[8,128,128]{2,1,0:T(8,128)S(1)}, f32[8,128,128]{2,1,0:T(8,128)}, u32[]{:S(2)}) %copy-start.1) | copy-done | bytes 524312
  2.9 0.0 copy-start.3
  2.9 0.7 copy-done.3
  3.6 0.0 copy-start.4
  3.6 0.7 copy-done.4
  4.2 0.0 copy-start.2
  4.2 0.0 copy-start.7
  4.2 24.9 %exchange.1 = (f32[2,16,128,128]{3,2,1,0:T(8,128)S(1)}, bf16[256,1024]{1,0:T(8,128)(2,1)S(1)}) custom-call(s32[16]{0:T(128)S(1)} %copy-done.4, s32[1,1024]{1,0:T(1,128)S(1)} %bitcast.4, f32[8,128,128]{2,1,0:T(8,128)S(1)} %copy-done.1, f32[2048,128]{1,0:T(8,128)S(1)} %copy-done), custom_call_target="tpu_custom_call" | custom-call | tf_op jit(solution)/shard_map/exchange/pallas_call | solution.py:384
  29.2 0.0 copy-start.5
  29.2 0.6 copy-done.5
  29.8 0.0 copy-start.6
  29.8 0.7 copy-done.6
  30.5 36.4 %sketch.1 = (f32[2048,256]{1,0:T(8,128)S(1)}, f32[2,4,4,8,1024]{4,3,2,1,0:T(8,128)S(1)}) custom-call(s32[3]{0:T(128)S(1)} %copy-done.5, f32[3]{0:T(128)S(1)} %copy-done.6, f32[2,16,128,128]{3,2,1,0:T(8,128)S(1)} %get-tuple-element.6.moved_ref, bf16[256,1024]{1,0:T(8,128)(2,1)S(1)} %get-tuple-element.7.table_ref), custom_call_target="tpu_custom_call" | custom-call | tf_op jit(solution)/shard_map/sketch/pallas_call | solution.py:410
  66.8 0.0 copy-done.2
  66.9 0.0 copy-done.7
  66.9 15.1 %finish.1 = (f32[2048,128]{1,0:T(8,128)}, f32[1,1024]{1,0:T(1,128)}) custom-call(s32[32]{0:T(128)S(1)} %bitcast.5, f32[256,1024]{1,0:T(8,128)S(1)} %bitcast.3, bf16[256,1024]{1,0:T(8,128)(2,1)S(1)} %get-tuple-element.7.table_ref, f32[2048,256]{1,0:T(8,128)S(1)} %get-tuple-element.9.sketch_ref, f32[8,64,64]{2,1,0:T(8,128)S(1)} %copy-done.2), custom_call_target="tpu_custom_call" | custom-call | tf_op jit(solution)/shard_map/finish/pallas_call | solution.py:435
Async XLA Ops:
  0.6 1.2 %copy-start = (f32[2048,128]{1,0:T(8,128)S(1)}, f32[2048,128]{1,0:T(8,128)}, u32[]{:S(2)}) copy-start(f32[2048,128]{1,0:T(8,128)} %factor_ref.1) | copy-start | bytes 3145732
  1.9 1.0 %copy-start.1 = (f32[8,128,128]{2,1,0:T(8,128)S(1)}, f32[8,128,128]{2,1,0:T(8,128)}, u32[]{:S(2)}) copy-start(f32[8,128,128]{2,1,0:T(8,128)} %gates_ref.1) | copy-start | bytes 1572868
  2.9 0.7 copy-start.3
  3.6 0.7 copy-start.4
  4.2 62.6 %copy-start.2 = (f32[8,64,64]{2,1,0:T(8,128)S(1)}, f32[8,64,64]{2,1,0:T(8,128)}, u32[]{:S(2)}) copy-start(f32[8,64,64]{2,1,0:T(8,128)} %bases_ref.1) | copy-start | bytes 393220
  4.2 62.6 %copy-start.7 = (s32[1,32]{1,0:T(1,128)S(1)}, s32[1,32]{1,0:T(1,128)}, u32[]{:S(2)}) copy-start(s32[1,32]{1,0:T(1,128)} %param.15) | copy-start | bytes 388
  29.2 0.7 copy-start.5
  29.8 0.7 copy-start.6
where the time goes:
time: 82.2 us; the launch traced here: 82 us
  Pallas kernels  76.4 us (93%)
  local copies, waits for them, and re-layouts  4.91 us (6%)
    pallas_call x1, Pallas kernels, per_device(): pl.pallas_call(functools.partial(sketch_kernel, groups), out_shape=[jax.S...  36.4 us
    pallas_call x1, Pallas kernels, per_device(): pl.pallas_call(functools.partial(exchange_kernel, count), out_shape=[jax....  24.9 us
    pallas_call x1, Pallas kernels, per_device(): pl.pallas_call(finish_kernel, out_shape=[jax.ShapeDtypeStruct((rows, widt...  15.1 us
    unnamed x16, local copies, waits for them, and re-layouts  4.91 us

commit v1 on v0

--- a/solution.py
+++ b/solution.py
@@ -381,6 +381,11 @@
     def dma(*shape):
         return pltpu.SemaphoreType.DMA(shape)
 
+    def stay(x):
+        return pltpu.with_memory_space_constraint(x, pltpu.HBM)
+
+    factor, gates, gate_layout, jump_masks, jump_rates = map(stay, (factor, gates, gate_layout, jump_masks, jump_rates))
+
     moved, table = pl.pallas_call(
         functools.partial(exchange_kernel, count),
         out_shape=[

time: 82.2 us -> 78.1 us (0.950)
  local copies, waits for them, and re-layouts: 4.91 us -> 0.69 us
    unnamed x16 -> x6, local copies, waits for them, and re-layouts: 4.91 us -> 0.69 us
where the time goes in v1:
time: 78.1 us; the launch traced here: 77.9 us
  Pallas kernels  76.5 us (98%)
    pallas_call x1, Pallas kernels, per_device(): pl.pallas_call(functools.partial(sketch_kernel, groups), out_shape=[jax.S...  36.6 us
    pallas_call x1, Pallas kernels, per_device(): pl.pallas_call(functools.partial(exchange_kernel, count), out_shape=[jax....  24.8 us
    pallas_call x1, Pallas kernels, per_device(): pl.pallas_call(finish_kernel, out_shape=[jax.ShapeDtypeStruct((rows, widt...  15.1 us

profile of v1, /device:TPU:0, one launch (start us, length us, event | category | flops | bytes accessed | tf_op | source)
XLA Modules:
  0.0 77.9 jit_solution(15763730439584761586)
XLA Ops:
  0.6 0.0 copy-start.1
  0.6 0.7 copy-done.1
  1.3 0.0 copy-start
  1.3 0.0 copy-start.2
  1.3 24.8 %exchange.1 = (f32[2,16,128,128]{3,2,1,0:T(8,128)S(1)}, bf16[256,1024]{1,0:T(8,128)(2,1)S(1)}) custom-call(s32[16]{0:T(128)} %layout_ref.1, s32[1,1024]{1,0:T(1,128)S(1)} %bitcast.4, f32[8,128,128]{2,1,0:T(8,128)} %gates_ref.1, f32[2048,128]{1,0:T(8,128)} %factor_ref.1), custom_call_target="tpu_custom_call" | custom-call | tf_op jit(solution)/shard_map/exchange/pallas_call | solution.py:389
  26.1 36.6 %sketch.1 = (f32[2048,256]{1,0:T(8,128)S(1)}, f32[2,4,4,8,1024]{4,3,2,1,0:T(8,128)S(1)}) custom-call(s32[3]{0:T(128)} %mask_ref.1, f32[3]{0:T(128)} %rate_ref.1, f32[2,16,128,128]{3,2,1,0:T(8,128)S(1)} %get-tuple-element.6.moved_ref, bf16[256,1024]{1,0:T(8,128)(2,1)S(1)} %get-tuple-element.7.table_ref), custom_call_target="tpu_custom_call" | custom-call | tf_op jit(solution)/shard_map/sketch/pallas_call | solution.py:415
  62.8 0.0 copy-done
  62.8 0.0 copy-done.2
  62.8 15.1 %finish.1 = (f32[2048,128]{1,0:T(8,128)}, f32[1,1024]{1,0:T(1,128)}) custom-call(s32[32]{0:T(128)S(1)} %bitcast.5, f32[256,1024]{1,0:T(8,128)S(1)} %bitcast.3, bf16[256,1024]{1,0:T(8,128)(2,1)S(1)} %get-tuple-element.7.table_ref, f32[2048,256]{1,0:T(8,128)S(1)} %get-tuple-element.9.sketch_ref, f32[8,64,64]{2,1,0:T(8,128)S(1)} %copy-done), custom_call_target="tpu_custom_call" | custom-call | tf_op jit(solution)/shard_map/finish/pallas_call | solution.py:440
Async XLA Ops:
  0.6 0.7 copy-start.1
  1.3 61.5 %copy-start = (f32[8,64,64]{2,1,0:T(8,128)S(1)}, f32[8,64,64]{2,1,0:T(8,128)}, u32[]{:S(2)}) copy-start(f32[8,64,64]{2,1,0:T(8,128)} %bases_ref.1) | copy-start | bytes 393220
  1.3 61.5 %copy-start.2 = (s32[1,32]{1,0:T(1,128)S(1)}, s32[1,32]{1,0:T(1,128)}, u32[]{:S(2)}) copy-start(s32[1,32]{1,0:T(1,128)} %param.15) | copy-start | bytes 388
